TPU v7x, 256 devices: a whole 4x4x8 slice. The times are simulated.
256 devices in a mesh: dp: 64 (over y, z_lo, x), ctx: 4 (over z_hi, core).
Axes of the slice: x: 4, y: 4, z: 8 (z_hi: 2, z_lo: 4; z = z_hi * 4 + z_lo), core: 2. Of those that a mesh axis runs over, the one named last changes fastest.
Arguments:
- hidden: bfloat16 [64, 512, 3584], P('dp', 'ctx'), may hold values from -6 to 6
- norm_gain: bfloat16 [3584], replicated, may hold values from 0.099609375 to 1.8984375
- w_query: bfloat16 [3584, 2048], P('dp'), may hold values from -0.09375 to 0.09375
- w_key: bfloat16 [3584, 512], P('dp'), may hold values from -0.09375 to 0.09375
- w_value: bfloat16 [3584, 512], P('dp'), may hold values from -0.09375 to 0.09375
- bias_query: bfloat16 [2048], replicated, may hold values from -4 to 4
- bias_key: bfloat16 [512], replicated, may hold values from -4 to 4
- bias_value: bfloat16 [512], replicated, may hold values from -4 to 4
- kv_blocks: int32 [16, 4, 4], P('ctx'), may hold values from 0 to 3, as said below
- block_counts: int32 [16, 4], P('ctx'), may hold values from 1 to 4, as said below
Outputs:
- attended: bfloat16 [64, 512, 2048], P('dp', 'ctx')
Inputs may be any that keep to these rules, and one draw needn't show every extreme that they name: Entry 0 of kv_blocks[h, b] is b itself; entries 1 to block_counts[h, b] - 1 are distinct blocks below b; later entries are valid block numbers that are not used. block_counts[h, b] is at most b + 1, and the last query block of every head has 4.
All inputs are finite; a program needn't handle non-finite values.
Results may differ from a plain program's by a relative error of at most 0.0053.
Values may be sent and summed in bfloat16 or wider, within the bound.
No kernel may reach another device: no remote copies, remote signals or barrier semaphores. Data moves between devices by JAX's collectives and lax.ppermute only.
A program may use at most 64 MiB of HBM per device.

v0:
```python
import jax
import jax.numpy as jnp
from jax import lax
from jax.sharding import PartitionSpec as P

KVH = 4
HEAD = 128
QHEADS = 16
BLOCK = 128
MAXB = 4
EPSILON = 1e-06
THETA = 1000000.0


def rms_norm(tokens, norm_gain):
    floats = tokens.astype(jnp.float32)
    meansq = jnp.mean(floats * floats, axis=-1, keepdims=True)
    return (floats * lax.rsqrt(meansq + EPSILON) * norm_gain.astype(jnp.float32)).astype(
        jnp.bfloat16
    )


def rotary(heads_in, position):
    half_size = heads_in.shape[-1] // 2
    exponent = jnp.arange(half_size, dtype=jnp.float32) * (2.0 / heads_in.shape[-1])
    inverse = jnp.power(jnp.float32(THETA), -exponent)
    angles = position[:, None] * inverse[None, :]
    cosine = jnp.cos(angles)[:, None, :]
    sine = jnp.sin(angles)[:, None, :]
    first = heads_in[..., :half_size]
    second = heads_in[..., half_size:]
    return jnp.concatenate(
        [first * cosine - second * sine, second * cosine + first * sine], axis=-1
    )


def finish_heads(summed, bias, heads, position, rotate_it):
    shaped = (summed + bias.astype(jnp.float32)).reshape(summed.shape[0], heads, HEAD)
    if rotate_it:
        shaped = rotary(shaped, position)
    return shaped.astype(jnp.bfloat16)


def fold_rows(source, pieces):
    return tuple((jnp.dot(source, piece, preferred_element_type=jnp.float32) for piece in pieces))


def sparse_head(queries, key_rows, value_rows, blocks, counts):
    nblocks = queries.shape[0] // BLOCK
    query_tiles = queries.reshape(nblocks, BLOCK, HEAD)
    key_tiles = key_rows.reshape(nblocks, BLOCK, HEAD)[blocks].reshape(nblocks, MAXB * BLOCK, HEAD)
    value_tiles = value_rows.reshape(nblocks, BLOCK, HEAD)[blocks].reshape(
        nblocks, MAXB * BLOCK, HEAD
    )
    scores = jnp.einsum(
        "qih,qjh->qij", query_tiles, key_tiles, preferred_element_type=jnp.float32
    ) * HEAD ** (-0.5)
    column = jnp.arange(MAXB * BLOCK)
    slot_of = column // BLOCK
    inside = column % BLOCK
    row_pos = jnp.arange(BLOCK)
    allowed = (slot_of[None, None, :] < counts[:, None, None]) & (
        (slot_of[None, None, :] > 0) | (inside[None, None, :] <= row_pos[None, :, None])
    )
    expo = jnp.where(allowed, jnp.exp(scores), jnp.float32(0.0))
    totals = jnp.sum(expo, axis=-1)
    probs = expo.astype(jnp.bfloat16)
    mixed = (
        jnp.einsum("qij,qjh->qih", probs, value_tiles, preferred_element_type=jnp.float32)
        / totals[..., None]
    )
    return mixed.astype(jnp.bfloat16).reshape(nblocks * BLOCK, HEAD)


def one_head(packed):
    return sparse_head(packed[0], packed[1], packed[2], packed[3], packed[4])


def body(
    hidden,
    norm_gain,
    w_query,
    w_key,
    w_value,
    bias_query,
    bias_key,
    bias_value,
    kv_blocks,
    block_counts,
):
    groups = lax.axis_size("ctx")
    device = lax.axis_index("ctx")
    tokens = hidden[0]
    local_rows = tokens.shape[0]
    seq_len = local_rows * groups
    heads_here = QHEADS // groups
    kv_here = KVH // groups
    width_query = heads_here * HEAD
    width_pair = kv_here * HEAD
    normed = rms_norm(tokens, norm_gain)
    sum_query, sum_key, sum_value = fold_rows(
        normed,
        (
            lax.all_gather(w_query, "dp", axis=0, tiled=True),
            lax.all_gather(w_key, "dp", axis=0, tiled=True),
            lax.all_gather(w_value, "dp", axis=0, tiled=True),
        ),
    )
    position = (device * local_rows + jnp.arange(local_rows, dtype=jnp.int32)).astype(jnp.float32)
    queries = finish_heads(sum_query, bias_query, QHEADS, position, True)
    key_rows = finish_heads(sum_key, bias_key, KVH, position, True)
    value_rows = finish_heads(sum_value, bias_value, KVH, position, False)
    query_send = queries.reshape(local_rows, groups, width_query)
    pair_send = jnp.concatenate([key_rows, value_rows], axis=2)
    query_got, pair_got = (
        lax.all_to_all(query_send, "ctx", split_axis=1, concat_axis=0, tiled=True),
        lax.all_to_all(pair_send, "ctx", split_axis=1, concat_axis=0, tiled=True),
    )
    queries = query_got.reshape(seq_len, heads_here, HEAD)
    key_rows = pair_got[:, 0, :width_pair].reshape(seq_len, kv_here, HEAD)
    value_rows = pair_got[:, 0, width_pair:].reshape(seq_len, kv_here, HEAD)
    group = heads_here // kv_here
    key_rows = jnp.repeat(key_rows, group, axis=1)
    value_rows = jnp.repeat(value_rows, group, axis=1)
    mixed = lax.map(
        one_head,
        (
            queries.transpose(1, 0, 2),
            key_rows.transpose(1, 0, 2),
            value_rows.transpose(1, 0, 2),
            kv_blocks,
            block_counts,
        ),
    )
    result = mixed.transpose(1, 0, 2).reshape(seq_len, 1, width_query)
    returned = lax.all_to_all(result, "ctx", split_axis=0, concat_axis=1, tiled=True)
    return returned.reshape(1, local_rows, QHEADS * HEAD)


def solution(mesh):
    placed = (
        P("dp", "ctx", None),
        P(),
        P("dp", None),
        P("dp", None),
        P("dp", None),
        P(),
        P(),
        P(),
        P("ctx", None, None),
        P("ctx", None),
    )
    return jax.shard_map(
        body, mesh=mesh, in_specs=placed, out_specs=P("dp", "ctx", None), check_vma=False
    )
```

profile of v0, /device:TPU:2, one launch (start us, length us, event | category | flops | bytes accessed | tf_op | source)
XLA Modules:
  0.0 1162.7 jit_solution(7236101994991256935)
XLA Ops:
  6.5 0.7 all-gather.8.cloned.1.call-update
  7.3 0.7 all-gather.6.cloned.1.call-update
  8.1 0.7 all-gather.4.cloned.1.call-update
  8.7 0.7 convert_element_type.56
  9.4 0.7 convert_element_type.54
  10.1 0.7 convert_element_type.60
  10.8 0.7 convert_element_type.59
  11.9 1.5 fusion.13
  13.4 350.6 %all-gather.8.cloned.1.call-done = bf16[3584,512]{1,0:T(8,128)(2,1)} async-done(((bf16[56,512]{1,0:T(8,128)(2,1)}), bf16[3584,512]{1,0:T(8,128)(2,1)}) %all-gather.8.cloned.1.call-update) | async-done | bytes 3670032 | tf_op jit(solution)/shard_map/all_gather | solution.py:106
  364.0 3.0 fusion.17
  367.1 349.2 %all-gather.6.cloned.1.call-done = bf16[3584,512]{1,0:T(8,128)(2,1)} async-done(((bf16[56,512]{1,0:T(8,128)(2,1)}), bf16[3584,512]{1,0:T(8,128)(2,1)}) %all-gather.6.cloned.1.call-update) | async-done | bytes 3670032 | tf_op jit(solution)/shard_map/all_gather | solution.py:105
  716.3 2.8 convolution_add_fusion.2
  719.4 0.9 pad_maximum_fusion.1
  720.3 4.1 all-to-all-start.1
  724.4 367.1 %all-gather.4.cloned.1.call-done = bf16[3584,2048]{1,0:T(8,128)(2,1)} async-done(((bf16[56,2048]{1,0:T(8,128)(2,1)}), bf16[3584,2048]{1,0:T(8,128)(2,1)}) %all-gather.4.cloned.1.call-update) | async-done | bytes 14680080 | tf_op jit(solution)/shard_map/all_gather | solution.py:104
  1091.4 7.3 convolution_add_fusion
  1099.3 0.8 pad_maximum_fusion
  1100.1 7.0 all-to-all-start
  1107.1 12.7 %all-to-all-done = bf16[128,4,512]{0,2,1:T(8,128)(2,1)S(1)} async-done(((bf16[128,4,512]{0,2,1:T(8,128)(2,1)}), bf16[128,4,512]{0,2,1:T(8,128)(2,1)S(1)}, u32[]{:S(2)}, u32[]{:S(2)}) %all-to-all-start) | async-done | bytes 524320 | tf_op jit(solution)/shard_map/all_to_all | solution.py:116
  1120.4 0.7 copy-done.1
  1121.1 15.8 %while.12 = (s32[]{:T(128)}, bf16[4,512,128]{1,2,0:T(8,128)(2,1)S(1)}, s32[4,4]{1,0:T(4,128)}, bf16[4,512,128]{2,1,0:T(8,128)(2,1)S(1)}, bf16[4,512,128]{2,1,0:T...) while((s32[]{:T(128)}, bf16[4,512,128]{1,2,0:T(8,128)(2,1)S(1)}, ...), condition=%wide.region_3.4_spmd, body=%wide.region_1.3_spmd.sunk | while | flops 135803952 | bytes 5920353 | solution.py:125
  1121.1 0.7 compare_select_fusion.2
  1123.3 0.7 fusion.45
  1125.0 0.7 compare_select_fusion.2
  1127.3 0.7 fusion.45
  1129.0 0.7 compare_select_fusion.2
  1131.2 0.7 fusion.45
  1133.0 0.7 compare_select_fusion.2
  1135.2 0.7 fusion.45
  1137.4 1.0 reduce
  1139.0 15.2 %all_to_all.48 = bf16[4,2,32768]{2,1,0:T(2,128)(2,1)S(1)} all-to-all(bf16[4,2,32768]{2,1,0:T(2,128)(2,1)S(1)} %reshape.302), channel_id=1, replica_groups=mesh['dp'=64,'ctx'=4] {'ctx'}, dimensions={0} | all-to-all | bytes 1048576 | tf_op jit(solution)/shard_map/all_to_all | solution.py:136
  1155.1 1.0 copy.42
  (88 shorter events, 13.9 us)
Async XLA Ops:
  6.5 357.5 %all-gather.8.cloned.1.call-start = ((), (), s32[]{:S(2)}) async-start(), calls=%async_computation.5 | async-start | bytes 3727360 | tf_op jit(solution)/shard_map/all_gather | solution.py:106
  7.3 709.0 %all-gather.6.cloned.1.call-start = ((), (), s32[]{:S(2)}) async-start(), calls=%async_computation.4 | async-start | bytes 3727360 | tf_op jit(solution)/shard_map/all_gather | solution.py:105
  8.0 1083.4 %all-gather.4.cloned.1.call-start = ((), (), s32[]{:S(2)}) async-start(), calls=%async_computation.3 | async-start | bytes 14909440 | tf_op jit(solution)/shard_map/all_gather | solution.py:104
  13.4 702.9 %copy-start = (bf16[1,128,3584]{2,1,0:T(8,128)(2,1)S(1)}, bf16[1,128,3584]{2,1,0:T(8,128)(2,1)}, u32[]{:S(2)}) copy-start(bf16[1,128,3584]{2,1,0:T(8,128)(2,1)} %param.12) | copy-start | bytes 2752516
  720.3 379.8 %all-to-all-start.1 = ((bf16[128,4,256]{2,0,1:T(8,128)(2,1)}), bf16[128,4,256]{2,0,1:T(8,128)(2,1)S(1)}, u32[]{:S(2)}, u32[]{:S(2)}) async-start(bf16[128,4,256]{2,0,1:T(8,128)(2,1)} %pad_maximum_fusion.1), calls=%async_computation.1 | async-start | bytes 524288 | tf_op jit(solution)/shard_map/all_to_all | solution.py:117
  1100.1 19.7 %all-to-all-start = ((bf16[128,4,512]{0,2,1:T(8,128)(2,1)}), bf16[128,4,512]{0,2,1:T(8,128)(2,1)S(1)}, u32[]{:S(2)}, u32[]{:S(2)}) async-start(bf16[128,4,512]{0,2,1:T(8,128)(2,1)} %bitcast.10), calls=%async_computation | async-start | bytes 1048576 | tf_op jit(solution)/shard_map/all_to_all | solution.py:116
  1120.0 1.0 copy-start.1
Sparse Core Ops, SparseCore 0:
  9.1 354.8 all-gather.7
  365.8 350.3 all-gather.5
  718.0 373.3 all-gather.3
where the time goes:
time: 1160 us
  waiting for transfers between devices  1080 us (93%)
  matrix products  16.3 us (1%)
  blocking collectives  15.2 us (1%)
  local copies, waits for them, and re-layouts  14.1 us (1%)
  between operations  13.3 us (1%)
    all_gather x1, waiting for transfers between devices, body(): lax.all_gather(w_query, 'dp', axis=0, tiled=True)  367 us
    all_gather x1, waiting for transfers between devices, body(): lax.all_gather(w_value, 'dp', axis=0, tiled=True)  351 us
    all_gather x1, waiting for transfers between devices, body(): lax.all_gather(w_key, 'dp', axis=0, tiled=True)  349 us
  transfers between devices with their start and end apart: 5, of which 4 were waited for; matrix products, arithmetic and copies ran while one was open for 2% of the time, Pallas kernels for 0%

commit v1 on v0

--- a/solution.py
+++ b/solution.py
@@ -10,6 +10,13 @@
 MAXB = 4
 EPSILON = 1e-06
 THETA = 1000000.0
+
+
+def gather_over(value, axis, along):
+    size = lax.axis_size(axis)
+    tiles = jnp.stack([value for _ in range(size)])
+    tiles = lax.all_to_all(tiles, axis, split_axis=0, concat_axis=0)
+    return jnp.concatenate(tiles, axis=along)
 
 
 def rms_norm(tokens, norm_gain):
@@ -103,7 +110,7 @@
         (
             lax.all_gather(w_query, "dp", axis=0, tiled=True),
             lax.all_gather(w_key, "dp", axis=0, tiled=True),
-            lax.all_gather(w_value, "dp", axis=0, tiled=True),
+            gather_over(w_value, "dp", 0),
         ),
     )
     position = (device * local_rows + jnp.arange(local_rows, dtype=jnp.int32)).astype(jnp.float32)

time: 1160 us -> 818 us (0.71)
  waiting for transfers between devices: 1080 us -> 726 us
    all_gather x1 -> x0, waiting for transfers between devices: 351 us -> none  [body(): lax.all_gather(w_value, 'dp', axis=0, tiled=True)]
    all_gather x1, waiting for transfers between devices: 349 us -> 251 us  [body(): lax.all_gather(w_key, 'dp', axis=0, tiled=True)]
    all_to_all x0 -> x1, waiting for transfers between devices: none -> 92.9 us  [gather_over(): tiles = lax.all_to_all(tiles, axis, split_axis=0, concat_axis=0)]
    all_to_all x0 -> x1, starting transfers between devices: none -> 12.4 us  [gather_over(): tiles = lax.all_to_all(tiles, axis, split_axis=0, concat_axis=0)]
where the time goes in v1:
time: 818 us; the launch traced here: 815 us
  waiting for transfers between devices  726 us (89%)
  starting transfers between devices  20.4 us (2%)
  local copies, waits for them, and re-layouts  17 us (2%)
  matrix products  15.9 us (2%)
  blocking collectives  15.2 us (2%)
  between operations  13.7 us (2%)
    all_gather x1, waiting for transfers between devices, body(): lax.all_gather(w_query, 'dp', axis=0, tiled=True)  368 us
    all_gather x1, waiting for transfers between devices, body(): lax.all_gather(w_key, 'dp', axis=0, tiled=True)  251 us
    all_to_all x1, waiting for transfers between devices, gather_over(): tiles = lax.all_to_all(tiles, axis, split_axis=0, concat_axis=0)  92.9 us
  transfers between devices with their start and end apart: 5, of which 4 were waited for; matrix products, arithmetic and copies ran while one was open for 2% of the time, Pallas kernels for 0%

profile of v1, /device:TPU:2, one launch (start us, length us, event | category | flops | bytes accessed | tf_op | source)
XLA Modules:
  0.0 815.2 jit_solution(4256833061810522466)
XLA Ops:
  6.5 0.7 all-gather.5.cloned.1.call-update
  7.3 0.7 all-gather.3.cloned.1.call-update
  8.0 2.9 stack.2
  10.9 12.4 %all-to-all-start.1 = ((bf16[64,56,512]{2,1,0:T(8,128)(2,1)}), bf16[64,56,512]{2,1,0:T(8,128)(2,1)}, u32[]{:S(2)}, u32[]{:S(2)}) async-start(bf16[64,56,512]{2,1,0:T(8,128)(2,1)} %stack.2), calls=%async_computation.1 | async-start | bytes 7340032 | tf_op jit(solution)/shard_map/all_to_all | solution.py:18
  24.1 92.9 %all-to-all-done.1 = bf16[64,56,512]{2,1,0:T(8,128)(2,1)} async-done(((bf16[64,56,512]{2,1,0:T(8,128)(2,1)}), bf16[64,56,512]{2,1,0:T(8,128)(2,1)}, u32[]{:S(2)}, u32[]{:S(2)}) %all-to-all-start.1) | async-done | bytes 3670048 | tf_op jit(solution)/shard_map/all_to_all | solution.py:18
  117.0 2.7 fusion.21
  119.8 251.0 %all-gather.5.cloned.1.call-done = bf16[3584,512]{1,0:T(8,128)(2,1)} async-done(((bf16[56,512]{1,0:T(8,128)(2,1)}), bf16[3584,512]{1,0:T(8,128)(2,1)}) %all-gather.5.cloned.1.call-update) | async-done | bytes 3670032 | tf_op jit(solution)/shard_map/all_gather | solution.py:112
  370.9 2.7 convolution_add_fusion.2
  374.0 0.9 pad_maximum_fusion.1
  374.8 3.4 all-to-all-start.2
  378.3 367.8 %all-gather.3.cloned.1.call-done = bf16[3584,2048]{1,0:T(8,128)(2,1)} async-done(((bf16[56,2048]{1,0:T(8,128)(2,1)}), bf16[3584,2048]{1,0:T(8,128)(2,1)}) %all-gather.3.cloned.1.call-update) | async-done | bytes 14680080 | tf_op jit(solution)/shard_map/all_gather | solution.py:111
  746.0 7.3 convolution_add_fusion
  753.8 0.8 pad_maximum_fusion
  754.7 4.6 all-to-all-start
  759.3 12.7 %all-to-all-done = bf16[128,4,512]{0,2,1:T(8,128)(2,1)S(1)} async-done(((bf16[128,4,512]{0,2,1:T(8,128)(2,1)}), bf16[128,4,512]{0,2,1:T(8,128)(2,1)S(1)}, u32[]{:S(2)}, u32[]{:S(2)}) %all-to-all-start) | async-done | bytes 524320 | tf_op jit(solution)/shard_map/all_to_all | solution.py:123
  772.6 0.7 copy-done.1
  773.3 15.8 %while.12 = (s32[]{:T(128)}, bf16[4,512,128]{1,2,0:T(8,128)(2,1)S(1)}, s32[4,4]{1,0:T(4,128)}, bf16[4,512,128]{2,1,0:T(8,128)(2,1)S(1)}, bf16[4,512,128]{2,1,0:T...) while((s32[]{:T(128)}, bf16[4,512,128]{1,2,0:T(8,128)(2,1)S(1)}, ...), condition=%wide.region_3.4_spmd, body=%wide.region_1.3_spmd.sunk | while | flops 135803952 | bytes 5920353 | solution.py:132
  773.3 0.7 compare_select_fusion.2
  774.7 0.6 gather_fusion.1
  775.5 0.7 fusion.52
  777.2 0.7 compare_select_fusion.2
  778.7 0.6 gather_fusion.1
  779.4 0.7 fusion.52
  781.2 0.7 compare_select_fusion.2
  782.7 0.6 gather_fusion.1
  783.4 0.7 fusion.52
  785.2 0.7 compare_select_fusion.2
  786.6 0.6 gather_fusion.1
  787.4 0.7 fusion.52
  789.6 1.0 reduce
  791.2 15.2 %all_to_all.53 = bf16[4,2,32768]{2,1,0:T(2,128)(2,1)S(1)} all-to-all(bf16[4,2,32768]{2,1,0:T(2,128)(2,1)S(1)} %reshape.321), channel_id=1, replica_groups=mesh['dp'=64,'ctx'=4] {'ctx'}, dimensions={0} | all-to-all | bytes 1048576 | tf_op jit(solution)/shard_map/all_to_all | solution.py:143
  807.3 1.0 copy.42
  (96 shorter events, 11.6 us)
Async XLA Ops:
  6.5 364.3 %all-gather.5.cloned.1.call-start = ((), (), s32[]{:S(2)}) async-start(), calls=%async_computation.5 | async-start | bytes 3727360 | tf_op jit(solution)/shard_map/all_gather | solution.py:112
  7.3 738.8 %all-gather.3.cloned.1.call-start = ((), (), s32[]{:S(2)}) async-start(), calls=%async_computation.4 | async-start | bytes 14909440 | tf_op jit(solution)/shard_map/all_gather | solution.py:111
  10.9 12.4 %copy-start.3 = (bf16[2048]{0:T(1024)(128)(2,1)S(1)}, bf16[2048]{0:T(1024)(128)(2,1)}, u32[]{:S(2)}) copy-start(bf16[2048]{0:T(1024)(128)(2,1)} %param.17) | copy-start | bytes 12292
  10.9 12.4 %copy-start.2 = (bf16[3584]{0:T(1024)(128)(2,1)S(1)}, bf16[3584]{0:T(1024)(128)(2,1)}, u32[]{:S(2)}) copy-start(bf16[3584]{0:T(1024)(128)(2,1)} %param.13) | copy-start | bytes 21508
  10.9 12.5 %copy-start.4 = (bf16[512]{0:T(512)(128)(2,1)S(1)}, bf16[512]{0:T(512)(128)(2,1)}, u32[]{:S(2)}) copy-start(bf16[512]{0:T(512)(128)(2,1)} %param.19) | copy-start | bytes 3076
  10.9 12.5 %copy-start.5 = (bf16[512]{0:T(512)(128)(2,1)S(1)}, bf16[512]{0:T(512)(128)(2,1)}, u32[]{:S(2)}) copy-start(bf16[512]{0:T(512)(128)(2,1)} %param.18) | copy-start | bytes 3076
  10.9 12.9 %copy-start = (bf16[1,128,3584]{2,1,0:T(8,128)(2,1)S(1)}, bf16[1,128,3584]{2,1,0:T(8,128)(2,1)}, u32[]{:S(2)}) copy-start(bf16[1,128,3584]{2,1,0:T(8,128)(2,1)} %param.12) | copy-start | bytes 2752516
  10.9 106.1 %all-to-all-start.1 = ((bf16[64,56,512]{2,1,0:T(8,128)(2,1)}), bf16[64,56,512]{2,1,0:T(8,128)(2,1)}, u32[]{:S(2)}, u32[]{:S(2)}) async-start(bf16[64,56,512]{2,1,0:T(8,128)(2,1)} %stack.2), calls=%async_computation.1 | async-start | bytes 7340032 | tf_op jit(solution)/shard_map/all_to_all | solution.py:18
  374.8 379.8 %all-to-all-start.2 = ((bf16[128,4,256]{2,0,1:T(8,128)(2,1)}), bf16[128,4,256]{2,0,1:T(8,128)(2,1)S(1)}, u32[]{:S(2)}, u32[]{:S(2)}) async-start(bf16[128,4,256]{2,0,1:T(8,128)(2,1)} %pad_maximum_fusion.1), calls=%async_computation.2 | async-start | bytes 524288 | tf_op jit(solution)/shard_map/all_to_all | solution.py:124
  754.7 17.3 %all-to-all-start = ((bf16[128,4,512]{0,2,1:T(8,128)(2,1)}), bf16[128,4,512]{0,2,1:T(8,128)(2,1)S(1)}, u32[]{:S(2)}, u32[]{:S(2)}) async-start(bf16[128,4,512]{0,2,1:T(8,128)(2,1)} %bitcast.9), calls=%async_computation | async-start | bytes 1048576 | tf_op jit(solution)/shard_map/all_to_all | solution.py:123
  772.2 1.0 copy-start.1
Sparse Core Ops, SparseCore 0:
  9.1 361.6 all-gather.4
  372.6 373.3 all-gather.2
